TPU v7x, 32 devices: a whole 2x2x4 slice. The times are simulated.
32 devices in a mesh: dp: 8 (over z, x), tensor: 4 (over y, core).
Axes of the slice: x: 2, y: 2, z: 4, core: 2. Of those that a mesh axis runs over, the one named last changes fastest.
Arguments:
- patches: bfloat16 [24, 2048, 1024], P('dp', 'tensor'), may hold values from -6 to 6
- cotangent: bfloat16 [24, 2048, 1024], P('dp', 'tensor'), may hold values from -6 to 6
- empty_slots: int32 [8], replicated, may hold values from 0 to 2
- dataset_id: int32 [24], replicated, may hold values from 0 to 5
- dataset_weight: int32 [6], replicated, may hold values from 1 to 8
- query_key_value_weight: bfloat16 [3, 1024, 1024], P(None, None, 'tensor'), may hold values from -0.25 to 0.25
- qv_bias: float32 [2, 1024], P(None, 'tensor'), may hold values from -3 to 3
- output_projection_weight: bfloat16 [1024, 1024], P('tensor'), may hold values from -0.75 to 0.75
- out_bias: float32 [1024], replicated, may hold values from -2 to 2
- up_projection_weight: bfloat16 [1024, 4096], P(None, 'tensor'), may hold values from -0.1875 to 0.1875
- up_bias: float32 [4096], P('tensor'), may hold values from -2 to 2
- down_projection_weight: bfloat16 [4096, 1024], P('tensor'), may hold values from -0.09375 to 0.09375
- down_bias: float32 [1024], replicated, may hold values from -2 to 2
- attn_gain: float32 [1024], replicated, may hold values from 0.5 to 1.5
- attn_shift: float32 [1024], replicated, may hold values from -1.5 to 1.5
- mlp_gain: float32 [1024], replicated, may hold values from 0.5 to 1.5
- mlp_shift: float32 [1024], replicated, may hold values from -1.5 to 1.5
Outputs:
- block_out: bfloat16 [24, 2048, 1024], P('dp', 'tensor')
- grad_patches: bfloat16 [24, 2048, 1024], P('dp', 'tensor')
- grad_qkv_weight: float32 [3, 1024, 1024], P(None, None, 'tensor')
- grad_qv_bias: float32 [2, 1024], P(None, 'tensor')
- grad_out_weight: float32 [1024, 1024], P('tensor')
- grad_out_bias: float32 [1024], replicated
- grad_up_weight: float32 [1024, 4096], P(None, 'tensor')
- grad_up_bias: float32 [4096], P('tensor')
- grad_down_weight: float32 [4096, 1024], P('tensor')
- grad_down_bias: float32 [1024], replicated
- grad_attn_gain: float32 [1024], replicated
- grad_attn_shift: float32 [1024], replicated
- sensitivity_feedforward_scale: float32 [1024], replicated
- grad_mlp_shift: float32 [1024], replicated
All inputs are finite; a program needn't handle non-finite values.
Results may differ from a plain program's by a relative error of at most 0.02.
Values may be sent and summed in bfloat16 or wider, within the bound.
No kernel may reach another device: no remote copies, remote signals or barrier semaphores. Data moves between devices by JAX's collectives and lax.ppermute only.
A program may use at most 256 MiB of HBM per device.

v0:
```python
import jax
import jax.numpy as jnp
from jax import lax
from jax.sharding import PartitionSpec as P

HD = 64
epsilon = 1e-05


def norm_rows(source, norm_gain, norm_shift):
    row_mean = jnp.mean(source, axis=-1, keepdims=True)
    centred = source - row_mean
    spread = jnp.mean(centred * centred, axis=-1, keepdims=True)
    return centred * lax.rsqrt(spread + epsilon) * norm_gain + norm_shift


def gelu_exact(pre_act):
    return jax.nn.gelu(pre_act, approximate=False)


def split_heads(array, head_count):
    return array.reshape(array.shape[0], array.shape[1], head_count, HD)


def attend_item(operands):
    queries, key_rows, values = operands
    length, head_count, head_size = queries.shape
    qblock = min(512, length)
    score_scale = head_size ** (-0.5)
    blocks = queries.reshape(length // qblock, qblock, head_count, head_size)

    def one_block(query_block):
        scores = (
            jnp.einsum("qhd,khd->hqk", query_block, key_rows, preferred_element_type=jnp.float32)
            * score_scale
        )
        row_top = jnp.max(scores, axis=-1, keepdims=True)
        exp_scores = jnp.exp(scores - row_top)
        row_total = jnp.sum(exp_scores, axis=-1, keepdims=True)
        attn_weights = (exp_scores / row_total).astype(jnp.bfloat16)
        attended = jnp.einsum(
            "hqk,khd->qhd", attn_weights, values, preferred_element_type=jnp.float32
        )
        return (attended.astype(jnp.bfloat16), (row_top + jnp.log(row_total))[:, :, 0])

    attended, log_total = lax.map(one_block, blocks)
    return (attended.reshape(length, head_count, head_size), log_total)


def attend_back(operands):
    queries, key_rows, values, grad_attended, log_total = operands
    length, head_count, head_size = queries.shape
    qblock = min(512, length)
    score_scale = head_size ** (-0.5)
    query_blocks = queries.reshape(length // qblock, qblock, head_count, head_size)
    grad_blocks = grad_attended.reshape(length // qblock, qblock, head_count, head_size)

    def one_block(carried, block_in):
        query_block, grad_block, lse_block = block_in
        scores = (
            jnp.einsum("qhd,khd->hqk", query_block, key_rows, preferred_element_type=jnp.float32)
            * score_scale
        )
        attn_weights = jnp.exp(scores - lse_block[:, :, None])
        grad_weights = jnp.einsum(
            "qhd,khd->hqk", grad_block, values, preferred_element_type=jnp.float32
        )
        grad_scores = attn_weights * (
            grad_weights - jnp.sum(attn_weights * grad_weights, axis=-1, keepdims=True)
        )
        grad_low = grad_scores.astype(jnp.bfloat16)
        sensitivity_questions = (
            jnp.einsum("hqk,khd->qhd", grad_low, key_rows, preferred_element_type=jnp.float32)
            * score_scale
        )
        key_acc = (
            carried[0]
            + jnp.einsum("hqk,qhd->khd", grad_low, query_block, preferred_element_type=jnp.float32)
            * score_scale
        )
        value_acc = carried[1] + jnp.einsum(
            "hqk,qhd->khd",
            attn_weights.astype(jnp.bfloat16),
            grad_block,
            preferred_element_type=jnp.float32,
        )
        return ((key_acc, value_acc), sensitivity_questions)

    zero_acc = jnp.zeros((length, head_count, head_size), jnp.float32)
    (grad_keys, grad_values), grad_queries = lax.scan(
        one_block, (zero_acc, zero_acc), (query_blocks, grad_blocks, log_total)
    )
    return (grad_queries.reshape(length, head_count, head_size), grad_keys, grad_values)


def shards(
    patches,
    cotangent,
    empty_slots,
    dataset_id,
    dataset_weight,
    query_key_value_weight,
    qv_bias,
    output_projection_weight,
    out_bias,
    up_projection_weight,
    up_bias,
    down_projection_weight,
    down_bias,
    attn_gain,
    attn_shift,
    mlp_gain,
    mlp_shift,
):
    number_format = jnp.float32
    half_type = jnp.bfloat16
    slot_count = patches.shape[0]
    group_slots = empty_slots.shape[0]
    slot_index = jnp.arange(group_slots * slot_count, dtype=jnp.int32) % slot_count
    filled = jnp.repeat(slot_count - empty_slots, slot_count)
    valid_all = (slot_index < filled).astype(number_format)
    table_hits = (
        dataset_id[:, None] == jnp.arange(dataset_weight.shape[0], dtype=jnp.int32)[None, :]
    )
    numerator = jnp.sum(jnp.where(table_hits, dataset_weight[None, :], 0), axis=1).astype(
        number_format
    )
    total_items = jnp.sum(valid_all)
    total_weight = jnp.sum(valid_all * numerator)
    multiplier_whole = valid_all * numerator * total_items / total_weight
    own_start = lax.axis_index("dp") * slot_count
    own_scale = lax.dynamic_slice_in_dim(multiplier_whole, own_start, slot_count)
    own_valid = lax.dynamic_slice_in_dim(valid_all, own_start, slot_count)
    inputs = patches.astype(number_format)
    normed = norm_rows(inputs, attn_gain, attn_shift).astype(half_type)
    normalized_every = lax.all_gather(normed, "tensor", axis=1, tiled=True)
    local_width = query_key_value_weight.shape[2]
    head_count = local_width // HD
    projected_rows = jnp.einsum(
        "owz,gzh->gowh",
        normalized_every,
        query_key_value_weight,
        preferred_element_type=number_format,
    )
    queries = split_heads((projected_rows[0] + qv_bias[0]).astype(half_type), head_count)
    key_rows = split_heads(projected_rows[1].astype(half_type), head_count)
    values = split_heads((projected_rows[2] + qv_bias[1]).astype(half_type), head_count)
    attended, log_total = lax.map(attend_item, (queries, key_rows, values))
    attended_matrix = attended.reshape(slot_count, attended.shape[1], local_width)
    attn_part = jnp.einsum(
        "ifz,zp->ifp",
        attended_matrix,
        output_projection_weight,
        preferred_element_type=number_format,
    )
    attn_rows = lax.psum_scatter(
        attn_part.astype(jnp.bfloat16), "tensor", scatter_dimension=1, tiled=True
    ).astype(jnp.float32)
    residual = inputs + attn_rows + out_bias
    normed_mlp = norm_rows(residual, mlp_gain, mlp_shift).astype(half_type)
    cot_scaled = cotangent.astype(number_format) * own_scale[:, None, None]
    cot_low = cot_scaled.astype(half_type)
    normalized_perceptron_every = lax.all_gather(normed_mlp, "tensor", axis=1, tiled=True)
    hidden_pre = (
        jnp.einsum(
            "jzb,bu->jzu",
            normalized_perceptron_every,
            up_projection_weight,
            preferred_element_type=number_format,
        )
        + up_bias
    )
    gelu_out, gelu_back = jax.vjp(gelu_exact, hidden_pre)
    latent_activations = gelu_out.astype(half_type)
    perceptron_portion = jnp.einsum(
        "vuc,cy->vuy",
        latent_activations,
        down_projection_weight,
        preferred_element_type=number_format,
    )
    mlp_rows = lax.psum_scatter(
        perceptron_portion.astype(jnp.bfloat16), "tensor", scatter_dimension=1, tiled=True
    ).astype(jnp.float32)
    output = ((residual + mlp_rows + down_bias) * own_valid[:, None, None]).astype(half_type)
    adjoint_for_each_layer = lax.all_gather(cot_low, "tensor", axis=1, tiled=True)
    hidden_gradient = jnp.einsum(
        "eph,wh->epw",
        adjoint_for_each_layer,
        down_projection_weight,
        preferred_element_type=number_format,
    )
    preactivation_gradient = gelu_back(hidden_gradient)[0].astype(half_type)
    down_gradient = jnp.einsum(
        "wuf,wul->fl",
        latent_activations,
        adjoint_for_each_layer,
        preferred_element_type=number_format,
    )
    up_gradient = jnp.einsum(
        "eug,eut->gt",
        normalized_perceptron_every,
        preactivation_gradient,
        preferred_element_type=number_format,
    )
    grad_up_bias = jnp.sum(preactivation_gradient.astype(number_format), axis=(0, 1))
    norm_portion = jnp.einsum(
        "jmn,hn->jmh",
        preactivation_gradient,
        up_projection_weight,
        preferred_element_type=number_format,
    )
    grad_normed_mlp = lax.psum_scatter(
        norm_portion.astype(jnp.bfloat16), "tensor", scatter_dimension=1, tiled=True
    ).astype(jnp.float32)
    mlp_norm_back = jax.vjp(norm_rows, residual, mlp_gain, mlp_shift)[1]
    grad_resid_norm, sensitivity_feedforward_scale, grad_mlp_shift = mlp_norm_back(grad_normed_mlp)
    grad_residual = cot_scaled + grad_resid_norm
    grad_out_bias = jnp.sum(grad_residual, axis=(0, 1))
    grad_down_bias = jnp.sum(cot_scaled, axis=(0, 1))
    residual_gradient_every = lax.all_gather(
        grad_residual.astype(half_type), "tensor", axis=1, tiled=True
    )
    grad_attended = jnp.einsum(
        "xmn,wn->xmw",
        residual_gradient_every,
        output_projection_weight,
        preferred_element_type=number_format,
    ).astype(half_type)
    grad_out = jnp.einsum(
        "ift,ifr->tr",
        attended_matrix,
        residual_gradient_every,
        preferred_element_type=number_format,
    )
    grad_queries, grad_keys, grad_values = lax.map(
        attend_back, (queries, key_rows, values, split_heads(grad_attended, head_count), log_total)
    )
    flat_shape = (slot_count, grad_queries.shape[1], local_width)
    projection_gradient = jnp.stack(
        [
            grad_queries.reshape(flat_shape).astype(half_type),
            grad_keys.reshape(flat_shape).astype(half_type),
            grad_values.reshape(flat_shape).astype(half_type),
        ]
    )
    query_key_value_gradient = jnp.einsum(
        "ktr,jktq->jrq", normalized_every, projection_gradient, preferred_element_type=number_format
    )
    grad_qv = jnp.stack(
        [
            jnp.sum(projection_gradient[0].astype(number_format), axis=(0, 1)),
            jnp.sum(projection_gradient[2].astype(number_format), axis=(0, 1)),
        ]
    )
    normed_part = jnp.einsum(
        "vbmk,vxk->bmx",
        projection_gradient,
        query_key_value_weight,
        preferred_element_type=number_format,
    )
    grad_normed = lax.psum_scatter(
        normed_part.astype(jnp.bfloat16), "tensor", scatter_dimension=1, tiled=True
    ).astype(jnp.float32)
    attn_norm_back = jax.vjp(norm_rows, inputs, attn_gain, attn_shift)[1]
    grad_input_norm, grad_attn_gain, grad_attn_shift = attn_norm_back(grad_normed)
    grad_inputs = (grad_residual + grad_input_norm).astype(half_type)
    summed = (
        lax.psum(query_key_value_gradient.astype(jnp.bfloat16), "dp").astype(jnp.float32),
        lax.psum(grad_qv.astype(jnp.bfloat16), "dp").astype(jnp.float32),
        lax.psum(grad_out.astype(jnp.bfloat16), "dp").astype(jnp.float32),
        lax.psum(up_gradient.astype(jnp.bfloat16), "dp").astype(jnp.float32),
        lax.psum(grad_up_bias.astype(jnp.bfloat16), "dp").astype(jnp.float32),
        lax.psum(down_gradient.astype(jnp.bfloat16), "dp").astype(jnp.float32),
    )
    small_sums = lax.psum(
        (
            grad_attn_gain,
            grad_attn_shift,
            sensitivity_feedforward_scale,
            grad_mlp_shift,
            grad_out_bias,
            grad_down_bias,
        ),
        ("dp", "tensor"),
    )
    return (
        output,
        grad_inputs,
        summed[0] / total_items,
        summed[1] / total_items,
        summed[2] / total_items,
        small_sums[4] / total_items,
        summed[3] / total_items,
        summed[4] / total_items,
        summed[5] / total_items,
        small_sums[5] / total_items,
        small_sums[0] / total_items,
        small_sums[1] / total_items,
        small_sums[2] / total_items,
        small_sums[3] / total_items,
    )


def solution(mesh):
    placed = (
        P("dp", "tensor", None),
        P("dp", "tensor", None),
        P(),
        P(),
        P(),
        P(None, None, "tensor"),
        P(None, "tensor"),
        P("tensor", None),
        P(),
        P(None, "tensor"),
        P("tensor"),
        P("tensor", None),
        P(),
        P(),
        P(),
        P(),
        P(),
    )
    return jax.shard_map(
        shards,
        mesh=mesh,
        in_specs=placed,
        out_specs=(
            P("dp", "tensor", None),
            P("dp", "tensor", None),
            P(None, None, "tensor"),
            P(None, "tensor"),
            P("tensor", None),
            P(),
            P(None, "tensor"),
            P("tensor"),
            P("tensor", None),
            P(),
            P(),
            P(),
            P(),
            P(),
        ),
        check_vma=False,
    )
```

profile of v0, /device:TPU:0, one launch (start us, length us, event | category | flops | bytes accessed | tf_op | source)
XLA Modules:
  0.0 1974.1 jit_solution(18060391247935320922)
XLA Ops:
  16.7 84.7 %all-gather.5.cloned.1.call-done = bf16[3,2048,1024]{2,1,0:T(8,128)(2,1)} async-done(((bf16[3,512,1024]{2,1,0:T(8,128)(2,1)}), bf16[3,2048,1024]{2,1,0:T(8,128)(2,1)}) %all-gather.5.cloned.1.call-update) | async-done | bytes 12582928 | tf_op jit(solution)/shard_map/all_gather | solution.py:136
  101.4 17.1 fusion.58
  123.4 11.4 fusion.102
  134.8 9.3 add_convert_fusion.3
  144.1 192.9 %while.54 = (s32[]{:T(128)}, bf16[3,2048,4,64]{1,3,2,0:T(8,128)(2,1)}, f32[3,4,4,512]{3,2,1,0:T(4,128)}, bf16[3,2048,4,64]{1,3,2,0:T(8,128)(2,1)}, bf16[3,2048,4...) while((s32[]{:T(128)}, ...), condition=%wide.region_7.8_spmd, body=%wide.region_2.7_spmd.sunk | while | flops 1111619584 | bytes 74055984 | solution.py:148
  152.4 47.4 %while.57 = (s32[]{:T(128)}, bf16[4,512,4,64]{1,3,2,0:T(8,128)(2,1)}, f32[4,4,512]{2,1,0:T(4,128)S(1)}, bf16[4,512,4,64]{1,3,2,0:T(8,128)(2,1)}, bf16[2048,4,64]...) while((s32[]{:T(128)}, bf16[4,512,4,64]{1,3,2,0:T(8,128)(2,1)}, ...), condition=%wide.region_6.6_spmd, body=%wide.region_3.5_spmd.sunk | while | flops 1111619584 | bytes 57213052 | solution.py:46
  216.6 47.4 %while.57 = (s32[]{:T(128)}, bf16[4,512,4,64]{1,3,2,0:T(8,128)(2,1)}, f32[4,4,512]{2,1,0:T(4,128)S(1)}, bf16[4,512,4,64]{1,3,2,0:T(8,128)(2,1)}, bf16[2048,4,64]...) while((s32[]{:T(128)}, bf16[4,512,4,64]{1,3,2,0:T(8,128)(2,1)}, ...), condition=%wide.region_6.6_spmd, body=%wide.region_3.5_spmd.sunk | while | flops 1111619584 | bytes 57213052 | solution.py:46
  280.8 47.4 %while.57 = (s32[]{:T(128)}, bf16[4,512,4,64]{1,3,2,0:T(8,128)(2,1)}, f32[4,4,512]{2,1,0:T(4,128)S(1)}, bf16[4,512,4,64]{1,3,2,0:T(8,128)(2,1)}, bf16[2048,4,64]...) while((s32[]{:T(128)}, bf16[4,512,4,64]{1,3,2,0:T(8,128)(2,1)}, ...), condition=%wide.region_6.6_spmd, body=%wide.region_3.5_spmd.sunk | while | flops 1111619584 | bytes 57213052 | solution.py:46
  336.9 10.1 convolution_convert_fusion.2
  347.1 99.1 %reduce-scatter.5.cloned.1.call-done = bf16[3,512,1024]{2,1,0:T(8,128)(2,1)} async-done(((bf16[3,2048,1024]{2,1,0:T(8,128)(2,1)}), bf16[3,512,1024]{2,1,0:T(8,128)(2,1)}) %reduce-scatter.5.cloned.1.call-update) | async-done | bytes 3145744 | tf_op jit(solution)/shard_map/reduce_scatter | solution.py:156
  465.1 73.9 %all-gather.7.cloned.1.call-done = bf16[3,2048,1024]{2,1,0:T(8,128)(2,1)} async-done(((bf16[3,512,1024]{2,1,0:T(8,128)(2,1)}), bf16[3,2048,1024]{2,1,0:T(8,128)(2,1)}) %all-gather.7.cloned.1.call-update) | async-done | bytes 12582928 | tf_op jit(solution)/shard_map/all_gather | solution.py:163
  539.1 29.6 %fusion.72 = (u8[2048,1024]{1,0:T(8,128)(4,1)}, u8[2048,1024]{1,0:T(8,128)(4,1)}, f32[3,2048,1024]{2,1,0:T(8,128)}) fusion(f32[1024]{0:T(1024)S(1)} %copy-done.41, bf16[3,2048,1024]{2,1,0:T(8,128)(2,1)} %all-gather.7.cloned.1.call-done, bf16[1024,1024]{1,0:T(8,128)(2,1)S(1)} %copy-done), kind=kOutput, calls=%fused_computation.128 | convolution fusion | flops 12968787968 | bytes 44044288 | tf_op jit(solution)/shard_map/jzb,bu->jzu/dot_general | solution.py:165
  568.7 61.6 %multiply_convert_fusion.1 = (bf16[3,2048,1024]{2,1,0:T(8,128)(2,1)}, f32[3,2048,1024]{2,1,0:T(8,128)}) fusion(f32[3,2048,1024]{2,1,0:T(8,128)} %get-tuple-element.412, f32[1024]{0:T(1024)S(1)} %copy-done.41, u8[2048,1024]{1,0:T(8,128)(4,1)} %get-tuple-element.313, u8[2048,1024]{1,0:T(8,128)(4,1)} %get-tuple-element.312), kind=kLoop, calls=%fused_computation.67 | loop fusion | flops 446693376 | bytes 67112960 | tf_op jit(solution)/shard_map/convert_element_type | solution.py:174
  630.3 32.6 %fusion.103 = (bf16[1024]{0:T(1024)(128)(2,1)}, bf16[3,2048,1024]{2,1,0:T(8,128)(2,1)}) fusion(f32[3,2048,1024]{2,1,0:T(8,128)} %get-tuple-element.399, bf16[3,2048,1024]{2,1,0:T(8,128)(2,1)} %all-gather.9.cloned.1.call-done, bf16[1024,1024]{1,0:T(8,128)(2,1)} %param.36, f32[3,2048,1024]{2,1,0:T(8,128)} %get-tuple-element.412, f32[1024]{0:T(1024)S(1)} %copy-done.41), kind=kOutput, calls=%fused_computation.192 | convolution fusion | flops 12985564160 | bytes 77600768 | tf_op jit(solution)/shard_map/eph,wh->epw/dot_general | solution.py:186
  662.9 20.4 %convolution_convert_fusion = bf16[3,2048,1024]{2,1,0:T(8,128)(2,1)} fusion(bf16[3,2048,1024]{2,1,0:T(8,128)(2,1)} %get-tuple-element.414, bf16[1024,1024]{1,0:T(8,128)(2,1)S(1)} %copy-done), kind=kOutput, calls=%fused_computation.105 | convolution fusion | flops 12891193344 | bytes 27262976 | tf_op jit(solution)/shard_map/jmn,hn->jmh/dot_general | solution.py:206
  684.8 21.3 %convolution_convert_fusion.1 = bf16[3,2048,1024]{2,1,0:T(8,128)(2,1)} fusion(bf16[3,2048,1024]{2,1,0:T(8,128)(2,1)} %get-tuple-element.398, bf16[1024,1024]{1,0:T(8,128)(2,1)S(1)} %copy-done.47), kind=kOutput, calls=%fused_computation.106 | convolution fusion | flops 12891193344 | bytes 27262976 | tf_op jit(solution)/shard_map/vuc,cy->vuy/dot_general | solution.py:175
  706.3 76.2 %reduce-scatter.9.cloned.1.call-done = bf16[3,512,1024]{2,1,0:T(8,128)(2,1)} async-done(((bf16[3,2048,1024]{2,1,0:T(8,128)(2,1)}), bf16[3,512,1024]{2,1,0:T(8,128)(2,1)}) %reduce-scatter.9.cloned.1.call-update) | async-done | bytes 3145744 | tf_op jit(solution)/shard_map/reduce_scatter | solution.py:212
  788.4 7.3 fusion.67
  795.7 88.3 %reduce-scatter.7.cloned.1.call-done = bf16[3,512,1024]{2,1,0:T(8,128)(2,1)} async-done(((bf16[3,2048,1024]{2,1,0:T(8,128)(2,1)}), bf16[3,512,1024]{2,1,0:T(8,128)(2,1)}) %reduce-scatter.7.cloned.1.call-update) | async-done | bytes 3145744 | tf_op jit(solution)/shard_map/reduce_scatter | solution.py:181
  884.0 10.3 fusion.100
  899.3 19.5 bitcast_convert_fusion.1
  918.9 19.0 bitcast_convert_fusion.2
  937.8 43.7 %all-gather.11.cloned.1.call-done = bf16[3,2048,1024]{2,1,0:T(8,128)(2,1)} async-done(((bf16[3,512,1024]{2,1,0:T(8,128)(2,1)}), bf16[3,2048,1024]{2,1,0:T(8,128)(2,1)}) %all-gather.11.cloned.1.call-update) | async-done | bytes 12582928 | tf_op jit(solution)/shard_map/all_gather | solution.py:220
  981.5 14.3 convolution_convert_fusion.3
  995.9 553.7 %while.56 = (s32[]{:T(128)}, bf16[3,2048,4,64]{1,3,2,0:T(8,128)(2,1)}, bf16[3,2048,4,64]{1,3,2,0:T(8,128)(2,1)}, bf16[3,2048,4,64]{1,3,2,0:T(8,128)(2,1)}, bf16[...) while((s32[]{:T(128)}, ...), condition=%wide.region_22.23_spmd, body=%wide.region_18.22_spmd.sunk | while | flops 2737436672 | bytes 246014544 | solution.py:235
  1010.8 158.2 %while.58 = (s32[]{:T(128)}, f32[2048,4,64]{0,2,1:T(8,128)}, f32[2048,4,64]{0,2,1:T(8,128)}, bf16[4,512,4,64]{1,3,2,0:T(8,128)(2,1)}, bf16[4,512,4,64]{1,3,2,0:T...) while((s32[]{:T(128)}, f32[2048,4,64]{0,2,1:T(8,128)}, ...), condition=%wide.region_21.21_spmd.clone, body=%wide.region_19.20_spmd.clone.sunk | while | flops 2737436672 | bytes 206102832 | solution.py:90
  1019.5 9.4 multiply_reduce_fusion.5
  1028.9 10.6 multiply_convert_fusion.4
  1039.4 6.9 fusion.152
  1059.0 9.4 multiply_reduce_fusion.5
  1068.4 10.6 multiply_convert_fusion.4
  1098.6 9.4 multiply_reduce_fusion.5
  1108.0 10.6 multiply_convert_fusion.4
  1138.1 9.4 multiply_reduce_fusion.5
  1147.5 10.6 multiply_convert_fusion.4
  1158.1 6.9 fusion.152
  1195.3 158.2 %while.58 = (s32[]{:T(128)}, f32[2048,4,64]{0,2,1:T(8,128)}, f32[2048,4,64]{0,2,1:T(8,128)}, bf16[4,512,4,64]{1,3,2,0:T(8,128)(2,1)}, bf16[4,512,4,64]{1,3,2,0:T...) while((s32[]{:T(128)}, f32[2048,4,64]{0,2,1:T(8,128)}, ...), condition=%wide.region_21.21_spmd.clone, body=%wide.region_19.20_spmd.clone.sunk | while | flops 2737436672 | bytes 206102832 | solution.py:90
  1203.9 9.4 multiply_reduce_fusion.5
  1213.3 10.6 multiply_convert_fusion.4
  1223.9 6.9 fusion.152
  1243.4 9.4 multiply_reduce_fusion.5
  1252.9 10.6 multiply_convert_fusion.4
  1263.4 6.9 fusion.152
  1283.0 9.4 multiply_reduce_fusion.5
  1292.4 10.6 multiply_convert_fusion.4
  1322.6 9.4 multiply_reduce_fusion.5
  1332.0 10.6 multiply_convert_fusion.4
  1379.8 158.2 %while.58 = (s32[]{:T(128)}, f32[2048,4,64]{0,2,1:T(8,128)}, f32[2048,4,64]{0,2,1:T(8,128)}, bf16[4,512,4,64]{1,3,2,0:T(8,128)(2,1)}, bf16[4,512,4,64]{1,3,2,0:T...) while((s32[]{:T(128)}, f32[2048,4,64]{0,2,1:T(8,128)}, ...), condition=%wide.region_21.21_spmd.clone, body=%wide.region_19.20_spmd.clone.sunk | while | flops 2737436672 | bytes 206102832 | solution.py:90
  1388.4 9.4 multiply_reduce_fusion.5
  1397.8 10.6 multiply_convert_fusion.4
  1427.9 9.4 multiply_reduce_fusion.5
  1437.4 10.6 multiply_convert_fusion.4
  1467.5 9.4 multiply_reduce_fusion.5
  1476.9 10.6 multiply_convert_fusion.4
  1507.0 9.4 multiply_reduce_fusion.5
  1516.4 10.6 multiply_convert_fusion.4
  1563.5 9.9 fusion.89
  1573.3 13.9 fusion.86
  1588.6 15.4 bitcast_convert_fusion
  1609.1 22.8 %all-reduce.1 = (bf16[2,256]{1,0:T(2,128)(2,1)S(1)}, bf16[1024]{0:T(1024)(128)(2,1)S(1)}) all-reduce(bf16[2,256]{1,0:T(2,128)(2,1)S(1)} %pad_maximum_fusion.7, bf16[1024]{0:T(1024)(128)(2,1)S(1)} %copy-done.45), channel_id=1, replica_groups=mesh['dp'=8,'tensor'=4] {'dp'}, use_global_device_ids=true, to_apply=%region_29.30 | all-reduce | flops 1536 | bytes 6144 | tf_op jit(solution)/shard_map/psum | solution.py:269
  1634.4 167.8 %all-reduce.5.cloned.1.call-done = (bf16[3,1024,256]{1,2,0:T(8,128)(2,1)}, bf16[256,1024]{1,0:T(8,128)(2,1)}, bf16[1024,1024]{1,0:T(8,128)(2,1)}, bf16[1024,1024]{1,0:T(8,128)(2,1)}) async-done(((bf16[3,1024,256]{1,2,0:T(8,128)(2,1)}, bf16[256,1024]{1,0:T(8,128)(2,1)}, bf16[1024,1024]{1,0:T(8,128)(2,1)}, bf16[1024,1024]{1,0:T(8,128)(2,1)}), (bf16[3,1024,256]{1,2,0:T(8,128)(2,1)}, ...) | async-done | bytes 6291472 | tf_op jit(solution)/shard_map/psum | solution.py:268
  1821.7 81.2 %reduce-scatter.11.cloned.1.call-done = bf16[3,512,1024]{2,1,0:T(8,128)(2,1)} async-done(((bf16[3,2048,1024]{2,1,0:T(8,128)(2,1)}), bf16[3,512,1024]{2,1,0:T(8,128)(2,1)}) %reduce-scatter.11.cloned.1.call-update) | async-done | bytes 3145744 | tf_op jit(solution)/shard_map/reduce_scatter | solution.py:261
  1912.9 39.7 %all-reduce = (f32[1024]{0:T(1024)S(1)}, f32[1024]{0:T(1024)S(1)}, f32[1024]{0:T(1024)S(1)}, f32[1024]{0:T(1024)S(1)}, f32[1024]{0:T(1024)S(1)}, /*index=5*/f32[1024]{0:T(1024)S(1)}) all-reduce(f32[1024]{0:T(1024)S(1)} %copy-done.37, f32[1024]{0:T(1024)S(1)} %copy-done.38, ...), channel_id=1, replica_groups=mesh['dp'=8,'tensor'=4] {'dp','tensor'}, use_global_device_ids=true, to_apply=%region_32.33 | all-reduce | flops 6144 | bytes 49152 | tf_op jit(solution)/shard_map/psum | solution.py:275
  1960.0 7.1 add_convert_fusion.1
  (502 shorter events, 582.8 us)
Async XLA Ops:
  7.2 531.9 %copy-start = (bf16[1024,1024]{1,0:T(8,128)(2,1)S(1)}, bf16[1024,1024]{1,0:T(8,128)(2,1)}, u32[]{:S(2)}) copy-start(bf16[1024,1024]{1,0:T(8,128)(2,1)} %param.34) | copy-start | bytes 6291460
  7.2 94.1 %all-gather.5.cloned.1.call-start = ((), (), s32[]{:S(2)}) async-start(), calls=%async_computation.4 | async-start | bytes 15728640 | tf_op jit(solution)/shard_map/all_gather | solution.py:136
  16.4 429.9 %reduce-scatter.5.cloned.1.call-start = ((), (), s32[]{:S(2)}) async-start(), calls=%async_computation.5 | async-start | bytes 15728640 | tf_op jit(solution)/shard_map/reduce_scatter | solution.py:156
  347.0 99.2 %copy-start.23 = (f32[1024]{0:T(1024)S(1)}, f32[1024]{0:T(1024)}, u32[]{:S(2)}) copy-start(f32[1024]{0:T(1024)} %param.33) | copy-start | bytes 12292
  347.1 106.7 %copy-start.32 = (f32[1024]{0:T(1024)S(1)}, f32[1024]{0:T(1024)}, u32[]{:S(2)}) copy-start(f32[1024]{0:T(1024)} %param.40) | copy-start | bytes 12292
  347.1 106.7 %copy-start.39 = (f32[1024]{0:T(1024)S(1)}, f32[1024]{0:T(1024)}, u32[]{:S(2)}) copy-start(f32[1024]{0:T(1024)} %param.41) | copy-start | bytes 12292
  347.1 192.0 %all-gather.7.cloned.1.call-start = ((), (), s32[]{:S(2)}) async-start(), calls=%async_computation.6 | async-start | bytes 15728640 | tf_op jit(solution)/shard_map/all_gather | solution.py:163
  456.8 82.3 %copy-start.41 = (f32[1024]{0:T(1024)S(1)}, f32[1024]{0:T(1024)}, u32[]{:S(2)}) copy-start(f32[1024]{0:T(1024)} %param.35) | copy-start | bytes 12292
  456.8 173.5 %all-gather.9.cloned.1.call-start = ((), (), s32[]{:S(2)}) async-start(), calls=%async_computation.8 | async-start | bytes 15728640 | tf_op jit(solution)/shard_map/all_gather | solution.py:185
  460.3 108.4 %copy-start.43 = (f32[3]{0:T(128)}, f32[3]{0:T(128)S(1)}, u32[]{:S(2)}) copy-start(f32[3]{0:T(128)S(1)} %dynamic_slice.47) | copy-start | bytes 40
  465.1 317.4 %reduce-scatter.9.cloned.1.call-start = ((), (), s32[]{:S(2)}) async-start(), calls=%async_computation.9 | async-start | bytes 15728640 | tf_op jit(solution)/shard_map/reduce_scatter | solution.py:212
  683.3 200.7 %reduce-scatter.7.cloned.1.call-start = ((), (), s32[]{:S(2)}) async-start(), calls=%async_computation.7 | async-start | bytes 15728640 | tf_op jit(solution)/shard_map/reduce_scatter | solution.py:181
  706.1 82.2 %copy-start.31 = (f32[3,512]{1,0:T(4,128)S(1)}, f32[3,512]{1,0:T(4,128)}, u32[]{:S(2)}) copy-start(f32[3,512]{1,0:T(4,128)} %copy-done.30) | copy-start | bytes 18436
  706.1 82.2 %copy-start.27 = (f32[3,512]{1,0:T(4,128)S(1)}, f32[3,512]{1,0:T(4,128)}, u32[]{:S(2)}) copy-start(f32[3,512]{1,0:T(4,128)} %copy-done.26) | copy-start | bytes 18436
  706.2 275.4 %all-gather.11.cloned.1.call-start = ((), (), s32[]{:S(2)}) async-start(), calls=%async_computation.10 | async-start | bytes 15728640 | tf_op jit(solution)/shard_map/all_gather | solution.py:220
  788.4 95.6 %copy-start.42 = (f32[1024]{0:T(1024)S(1)}, f32[1024]{0:T(1024)}, u32[]{:S(2)}) copy-start(f32[1024]{0:T(1024)} %param.37) | copy-start | bytes 12292
  788.4 95.6 %copy-start.44 = (f32[3]{0:T(128)S(1)}, f32[3]{0:T(128)}, u32[]{:S(2)}) copy-start(f32[3]{0:T(128)} %copy-done.43) | copy-start | bytes 40
  899.2 902.9 %all-reduce.5.cloned.1.call-start = ((), (), s32[]{:S(2)}) async-start(), calls=%async_computation.12 | async-start | bytes 12582912 | tf_op jit(solution)/shard_map/psum | solution.py:268
  918.9 62.7 %copy-start.19 = (bf16[256,1024]{1,0:T(8,128)(2,1)S(1)}, bf16[256,1024]{1,0:T(8,128)(2,1)}, u32[]{:S(2)}) copy-start(bf16[256,1024]{1,0:T(8,128)(2,1)} %param.32) | copy-start | bytes 1572868
  1019.4 9.4 copy-start.4
  1028.9 17.5 copy-start.6
  1039.4 6.9 copy-start.2
  1059.0 9.4 copy-start.4
  1068.4 17.5 copy-start.6
  1098.5 9.4 copy-start.4
  1108.0 17.5 copy-start.6
  1118.5 6.9 copy-start.2
  1138.1 9.4 copy-start.4
  1147.5 17.5 copy-start.6
  1169.0 8.2 copy-start.5
  1203.9 9.4 copy-start.4
  1213.3 17.5 copy-start.6
  1243.4 9.4 copy-start.4
  1252.9 17.5 copy-start.6
  1283.0 9.4 copy-start.4
  1292.4 17.5 copy-start.6
  1322.5 9.4 copy-start.4
  1332.0 17.5 copy-start.6
  1342.5 6.9 copy-start.2
  1353.5 8.2 copy-start.5
  1388.4 9.4 copy-start.4
  1397.8 17.5 copy-start.6
  1427.9 9.4 copy-start.4
  1437.3 17.5 copy-start.6
  1467.5 9.4 copy-start.4
  1476.9 17.5 copy-start.6
  1507.0 9.4 copy-start.4
  1516.4 17.5 copy-start.6
  1537.9 8.2 copy-start.5
  1563.5 9.9 copy-start.15
  1563.5 9.9 copy-start.16
  1563.5 9.9 copy-start.17
  1587.3 315.7 %reduce-scatter.11.cloned.1.call-start = ((), (), s32[]{:S(2)}) async-start(), calls=%async_computation.11 | async-start | bytes 15728640 | tf_op jit(solution)/shard_map/reduce_scatter | solution.py:261
  1802.1 8.2 copy-start.20
  1806.4 11.7 copy-start.18
  1812.1 90.8 %copy-start.22 = (f32[3,512]{1,0:T(4,128)S(1)}, f32[3,512]{1,0:T(4,128)}, u32[]{:S(2)}) copy-start(f32[3,512]{1,0:T(4,128)} %copy-done.21) | copy-start | bytes 18436
  1812.1 90.8 %copy-start.34 = (f32[1024]{0:T(1024)S(1)}, f32[1024]{0:T(1024)}, u32[]{:S(2)}) copy-start(f32[1024]{0:T(1024)} %param.38) | copy-start | bytes 12292
  1818.0 89.3 %copy-start.29 = (f32[3,512]{1,0:T(4,128)S(1)}, f32[3,512]{1,0:T(4,128)}, u32[]{:S(2)}) copy-start(f32[3,512]{1,0:T(4,128)} %copy-done.28) | copy-start | bytes 18436
  1818.0 89.4 %copy-start.25 = (f32[3,512]{1,0:T(4,128)S(1)}, f32[3,512]{1,0:T(4,128)}, u32[]{:S(2)}) copy-start(f32[3,512]{1,0:T(4,128)} %copy-done.24) | copy-start | bytes 18436
  1821.7 91.2 %copy-start.35 = (f32[1024]{0:T(1024)S(1)}, f32[1024]{0:T(1024)}, u32[]{:S(2)}) copy-start(f32[1024]{0:T(1024)} %get-tuple-element.318) | copy-start | bytes 12292
  1821.7 91.2 %copy-start.36 = (f32[1024]{0:T(1024)S(1)}, f32[1024]{0:T(1024)}, u32[]{:S(2)}) copy-start(f32[1024]{0:T(1024)} %get-tuple-element.314) | copy-start | bytes 12292
  1821.7 91.2 %copy-start.37 = (f32[1024]{0:T(1024)S(1)}, f32[1024]{0:T(1024)}, u32[]{:S(2)}) copy-start(f32[1024]{0:T(1024)} %get-tuple-element.396) | copy-start | bytes 12292
  1821.7 91.2 %copy-start.38 = (f32[1024]{0:T(1024)S(1)}, f32[1024]{0:T(1024)}, u32[]{:S(2)}) copy-start(f32[1024]{0:T(1024)} %get-tuple-element.411) | copy-start | bytes 12292
  1960.0 7.1 copy-start.1
  (65 other events, 232.1 us)
Sparse Core Ops, SparseCore 0:
  16.5 84.7 all-gather.4
  347.2 99.0 reduce-scatter.4
  456.9 82.0 all-gather.6
  540.5 82.0 all-gather.8
  683.4 99.0 reduce-scatter.8
  785.0 99.0 reduce-scatter.6
  899.4 82.1 all-gather.10
  1587.4 214.7 all-reduce.4
  1804.9 97.9 reduce-scatter.10
where the time goes:
time: 1990 us; the launch traced here: 1970 us
  waiting for transfers between devices  715 us (36%)
  matrix products  649 us (33%)
  other arithmetic  334 us (17%)
  local copies, waits for them, and re-layouts  196 us (10%)
  blocking collectives  62.6 us (3%)
    psum x1, waiting for transfers between devices, shards(): lax.psum(query_key_value_gradient.astype(jnp.bfloat16), 'dp')  168 us
    convert_element_type x12, other arithmetic, one_block(): grad_low = grad_scores.astype(jnp.bfloat16)  127 us
    dot_general x12, matrix products, one_block(): jnp.einsum('qhd,khd->hqk', grad_block, values, preferred_element_type=jnp...  113 us
    reduce_scatter x1, waiting for transfers between devices, shards(): lax.psum_scatter(attn_part.astype(jnp.bfloat16), 'tensor', scatter_dimens...  99.1 us
    reduce_scatter x1, waiting for transfers between devices, shards(): lax.psum_scatter(perceptron_portion.astype(jnp.bfloat16), 'tensor', scatt...  88.3 us
    all_gather x1, waiting for transfers between devices, shards(): normalized_every = lax.all_gather(normed, 'tensor', axis=1, tiled=True)  84.7 us
    dot_general x12, matrix products, one_block(): jnp.einsum('hqk,khd->qhd', grad_low, key_rows, preferred_element_type=jnp...  82.8 us
    dot_general x24, matrix products, one_block(): jnp.einsum('qhd,khd->hqk', query_block, key_rows, preferred_element_type=...  82.5 us
  transfers between devices with their start and end apart: 9, of which 8 were waited for; matrix products, arithmetic and copies ran while one was open for 11% of the time, Pallas kernels for 0%

commit v1 on v0

--- a/solution.py
+++ b/solution.py
@@ -273,15 +273,18 @@
         lax.psum(down_gradient.astype(jnp.bfloat16), "dp").astype(jnp.float32),
     )
     small_sums = lax.psum(
-        (
-            grad_attn_gain,
-            grad_attn_shift,
-            sensitivity_feedforward_scale,
-            grad_mlp_shift,
-            grad_out_bias,
-            grad_down_bias,
+        lax.psum(
+            (
+                grad_attn_gain,
+                grad_attn_shift,
+                sensitivity_feedforward_scale,
+                grad_mlp_shift,
+                grad_out_bias,
+                grad_down_bias,
+            ),
+            "tensor",
         ),
-        ("dp", "tensor"),
+        "dp",
     )
     return (
         output,

time: 1990 us -> 1990 us (level)
    psum x0 -> x1, blocking collectives: none -> 37.2 us  [shards(): lax.psum(lax.psum((grad_attn_gain, grad_attn_shift, sensitivity_feedforwa...]
    psum x1, blocking collectives: 39.7 us -> 10.3 us  [shards(): lax.psum((grad_attn_gain, grad_attn_shift, sensitivity_feedforward_scale,...]
where the time goes in v1:
time: 1990 us; the launch traced here: 1980 us
  waiting for transfers between devices  715 us (36%)
  matrix products  647 us (33%)
  other arithmetic  335 us (17%)
  local copies, waits for them, and re-layouts  196 us (10%)
  blocking collectives  70.3 us (4%)
    psum x1, waiting for transfers between devices, shards(): lax.psum(query_key_value_gradient.astype(jnp.bfloat16), 'dp')  168 us
    convert_element_type x12, other arithmetic, one_block(): grad_low = grad_scores.astype(jnp.bfloat16)  127 us
    dot_general x12, matrix products, one_block(): jnp.einsum('qhd,khd->hqk', grad_block, values, preferred_element_type=jnp...  111 us
    reduce_scatter x1, waiting for transfers between devices, shards(): lax.psum_scatter(attn_part.astype(jnp.bfloat16), 'tensor', scatter_dimens...  99.2 us
    reduce_scatter x1, waiting for transfers between devices, shards(): lax.psum_scatter(perceptron_portion.astype(jnp.bfloat16), 'tensor', scatt...  88.3 us
    all_gather x1, waiting for transfers between devices, shards(): normalized_every = lax.all_gather(normed, 'tensor', axis=1, tiled=True)  84.7 us
    dot_general x12, matrix products, one_block(): jnp.einsum('hqk,khd->qhd', grad_low, key_rows, preferred_element_type=jnp...  82.8 us
    dot_general x24, matrix products, one_block(): jnp.einsum('qhd,khd->hqk', query_block, key_rows, preferred_element_type=...  82.5 us
  transfers between devices with their start and end apart: 9, of which 8 were waited for; matrix products, arithmetic and copies ran while one was open for 11% of the time, Pallas kernels for 0%

profile of v1, /device:TPU:0, one launch (start us, length us, event | category | flops | bytes accessed | tf_op | source)
XLA Modules:
  0.0 1979.8 jit_solution(14099493927202814894)
XLA Ops:
  16.7 84.7 %all-gather.5.cloned.1.call-done = bf16[3,2048,1024]{2,1,0:T(8,128)(2,1)} async-done(((bf16[3,512,1024]{2,1,0:T(8,128)(2,1)}), bf16[3,2048,1024]{2,1,0:T(8,128)(2,1)}) %all-gather.5.cloned.1.call-update) | async-done | bytes 12582928 | tf_op jit(solution)/shard_map/all_gather | solution.py:136
  101.4 17.0 fusion.58
  123.3 11.4 fusion.102
  134.7 9.3 add_convert_fusion.3
  144.0 192.8 %while.54 = (s32[]{:T(128)}, bf16[3,2048,4,64]{1,3,2,0:T(8,128)(2,1)}, f32[3,4,4,512]{3,2,1,0:T(4,128)}, bf16[3,2048,4,64]{1,3,2,0:T(8,128)(2,1)}, bf16[3,2048,4...) while((s32[]{:T(128)}, ...), condition=%wide.region_7.8_spmd, body=%wide.region_2.7_spmd.sunk | while | flops 1111619584 | bytes 74055984 | solution.py:148
  152.3 47.4 %while.57 = (s32[]{:T(128)}, bf16[4,512,4,64]{1,3,2,0:T(8,128)(2,1)}, f32[4,4,512]{2,1,0:T(4,128)S(1)}, bf16[4,512,4,64]{1,3,2,0:T(8,128)(2,1)}, bf16[2048,4,64]...) while((s32[]{:T(128)}, bf16[4,512,4,64]{1,3,2,0:T(8,128)(2,1)}, ...), condition=%wide.region_6.6_spmd, body=%wide.region_3.5_spmd.sunk | while | flops 1111619584 | bytes 57213052 | solution.py:46
  216.5 47.4 %while.57 = (s32[]{:T(128)}, bf16[4,512,4,64]{1,3,2,0:T(8,128)(2,1)}, f32[4,4,512]{2,1,0:T(4,128)S(1)}, bf16[4,512,4,64]{1,3,2,0:T(8,128)(2,1)}, bf16[2048,4,64]...) while((s32[]{:T(128)}, bf16[4,512,4,64]{1,3,2,0:T(8,128)(2,1)}, ...), condition=%wide.region_6.6_spmd, body=%wide.region_3.5_spmd.sunk | while | flops 1111619584 | bytes 57213052 | solution.py:46
  280.7 47.4 %while.57 = (s32[]{:T(128)}, bf16[4,512,4,64]{1,3,2,0:T(8,128)(2,1)}, f32[4,4,512]{2,1,0:T(4,128)S(1)}, bf16[4,512,4,64]{1,3,2,0:T(8,128)(2,1)}, bf16[2048,4,64]...) while((s32[]{:T(128)}, bf16[4,512,4,64]{1,3,2,0:T(8,128)(2,1)}, ...), condition=%wide.region_6.6_spmd, body=%wide.region_3.5_spmd.sunk | while | flops 1111619584 | bytes 57213052 | solution.py:46
  336.8 10.1 convolution_convert_fusion.2
  347.0 99.2 %reduce-scatter.5.cloned.1.call-done = bf16[3,512,1024]{2,1,0:T(8,128)(2,1)} async-done(((bf16[3,2048,1024]{2,1,0:T(8,128)(2,1)}), bf16[3,512,1024]{2,1,0:T(8,128)(2,1)}) %reduce-scatter.5.cloned.1.call-update) | async-done | bytes 3145744 | tf_op jit(solution)/shard_map/reduce_scatter | solution.py:156
  465.1 73.8 %all-gather.7.cloned.1.call-done = bf16[3,2048,1024]{2,1,0:T(8,128)(2,1)} async-done(((bf16[3,512,1024]{2,1,0:T(8,128)(2,1)}), bf16[3,2048,1024]{2,1,0:T(8,128)(2,1)}) %all-gather.7.cloned.1.call-update) | async-done | bytes 12582928 | tf_op jit(solution)/shard_map/all_gather | solution.py:163
  539.0 29.6 %fusion.72 = (u8[2048,1024]{1,0:T(8,128)(4,1)}, u8[2048,1024]{1,0:T(8,128)(4,1)}, f32[3,2048,1024]{2,1,0:T(8,128)}) fusion(f32[1024]{0:T(1024)S(1)} %copy-done.41, bf16[3,2048,1024]{2,1,0:T(8,128)(2,1)} %all-gather.7.cloned.1.call-done, bf16[1024,1024]{1,0:T(8,128)(2,1)S(1)} %copy-done), kind=kOutput, calls=%fused_computation.128 | convolution fusion | flops 12968787968 | bytes 44044288 | tf_op jit(solution)/shard_map/jzb,bu->jzu/dot_general | solution.py:165
  568.6 61.5 %multiply_convert_fusion.1 = (bf16[3,2048,1024]{2,1,0:T(8,128)(2,1)}, f32[3,2048,1024]{2,1,0:T(8,128)}) fusion(f32[3,2048,1024]{2,1,0:T(8,128)} %get-tuple-element.418, f32[1024]{0:T(1024)S(1)} %copy-done.41, u8[2048,1024]{1,0:T(8,128)(4,1)} %get-tuple-element.313, u8[2048,1024]{1,0:T(8,128)(4,1)} %get-tuple-element.312), kind=kLoop, calls=%fused_computation.67 | loop fusion | flops 446693376 | bytes 67112960 | tf_op jit(solution)/shard_map/convert_element_type | solution.py:174
  630.1 32.6 %fusion.103 = (bf16[1024]{0:T(1024)(128)(2,1)}, bf16[3,2048,1024]{2,1,0:T(8,128)(2,1)}) fusion(f32[3,2048,1024]{2,1,0:T(8,128)} %get-tuple-element.405, bf16[3,2048,1024]{2,1,0:T(8,128)(2,1)} %all-gather.9.cloned.1.call-done, bf16[1024,1024]{1,0:T(8,128)(2,1)} %param.36, f32[3,2048,1024]{2,1,0:T(8,128)} %get-tuple-element.418, f32[1024]{0:T(1024)S(1)} %copy-done.41), kind=kOutput, calls=%fused_computation.192 | convolution fusion | flops 12985564160 | bytes 77600768 | tf_op jit(solution)/shard_map/eph,wh->epw/dot_general | solution.py:186
  662.7 20.3 %convolution_convert_fusion = bf16[3,2048,1024]{2,1,0:T(8,128)(2,1)} fusion(bf16[3,2048,1024]{2,1,0:T(8,128)(2,1)} %get-tuple-element.420, bf16[1024,1024]{1,0:T(8,128)(2,1)S(1)} %copy-done), kind=kOutput, calls=%fused_computation.105 | convolution fusion | flops 12891193344 | bytes 27262976 | tf_op jit(solution)/shard_map/jmn,hn->jmh/dot_general | solution.py:206
  684.6 21.2 %convolution_convert_fusion.1 = bf16[3,2048,1024]{2,1,0:T(8,128)(2,1)} fusion(bf16[3,2048,1024]{2,1,0:T(8,128)(2,1)} %get-tuple-element.404, bf16[1024,1024]{1,0:T(8,128)(2,1)S(1)} %copy-done.47), kind=kOutput, calls=%fused_computation.106 | convolution fusion | flops 12891193344 | bytes 27262976 | tf_op jit(solution)/shard_map/vuc,cy->vuy/dot_general | solution.py:175
  706.1 76.2 %reduce-scatter.9.cloned.1.call-done = bf16[3,512,1024]{2,1,0:T(8,128)(2,1)} async-done(((bf16[3,2048,1024]{2,1,0:T(8,128)(2,1)}), bf16[3,512,1024]{2,1,0:T(8,128)(2,1)}) %reduce-scatter.9.cloned.1.call-update) | async-done | bytes 3145744 | tf_op jit(solution)/shard_map/reduce_scatter | solution.py:212
  788.2 7.3 fusion.67
  795.4 88.3 %reduce-scatter.7.cloned.1.call-done = bf16[3,512,1024]{2,1,0:T(8,128)(2,1)} async-done(((bf16[3,2048,1024]{2,1,0:T(8,128)(2,1)}), bf16[3,512,1024]{2,1,0:T(8,128)(2,1)}) %reduce-scatter.7.cloned.1.call-update) | async-done | bytes 3145744 | tf_op jit(solution)/shard_map/reduce_scatter | solution.py:181
  883.8 10.3 fusion.100
  899.1 19.5 bitcast_convert_fusion.1
  918.6 19.0 bitcast_convert_fusion.2
  937.6 43.7 %all-gather.11.cloned.1.call-done = bf16[3,2048,1024]{2,1,0:T(8,128)(2,1)} async-done(((bf16[3,512,1024]{2,1,0:T(8,128)(2,1)}), bf16[3,2048,1024]{2,1,0:T(8,128)(2,1)}) %all-gather.11.cloned.1.call-update) | async-done | bytes 12582928 | tf_op jit(solution)/shard_map/all_gather | solution.py:220
  981.3 14.3 convolution_convert_fusion.3
  995.6 551.7 %while.56 = (s32[]{:T(128)}, bf16[3,2048,4,64]{1,3,2,0:T(8,128)(2,1)}, bf16[3,2048,4,64]{1,3,2,0:T(8,128)(2,1)}, bf16[3,2048,4,64]{1,3,2,0:T(8,128)(2,1)}, bf16[...) while((s32[]{:T(128)}, ...), condition=%wide.region_22.23_spmd, body=%wide.region_18.22_spmd.sunk | while | flops 2737436672 | bytes 246014544 | solution.py:235
  1010.5 157.5 %while.58 = (s32[]{:T(128)}, f32[2048,4,64]{0,2,1:T(8,128)}, f32[2048,4,64]{0,2,1:T(8,128)}, bf16[4,512,4,64]{1,3,2,0:T(8,128)(2,1)}, bf16[4,512,4,64]{1,3,2,0:T...) while((s32[]{:T(128)}, f32[2048,4,64]{0,2,1:T(8,128)}, ...), condition=%wide.region_21.21_spmd.clone, body=%wide.region_19.20_spmd.clone.sunk | while | flops 2737436672 | bytes 206102832 | solution.py:90
  1019.2 9.2 multiply_reduce_fusion.5
  1028.4 10.5 multiply_convert_fusion.4
  1039.0 6.9 fusion.152
  1058.6 9.2 multiply_reduce_fusion.5
  1067.8 10.5 multiply_convert_fusion.4
  1078.4 6.9 fusion.152
  1097.9 9.2 multiply_reduce_fusion.5
  1107.2 10.5 multiply_convert_fusion.4
  1137.3 9.2 multiply_reduce_fusion.5
  1146.6 10.5 multiply_convert_fusion.4
  1157.1 6.9 fusion.152
  1194.3 157.5 %while.58 = (s32[]{:T(128)}, f32[2048,4,64]{0,2,1:T(8,128)}, f32[2048,4,64]{0,2,1:T(8,128)}, bf16[4,512,4,64]{1,3,2,0:T(8,128)(2,1)}, bf16[4,512,4,64]{1,3,2,0:T...) while((s32[]{:T(128)}, f32[2048,4,64]{0,2,1:T(8,128)}, ...), condition=%wide.region_21.21_spmd.clone, body=%wide.region_19.20_spmd.clone.sunk | while | flops 2737436672 | bytes 206102832 | solution.py:90
  1202.9 9.2 multiply_reduce_fusion.5
  1212.2 10.5 multiply_convert_fusion.4
  1242.3 9.2 multiply_reduce_fusion.5
  1251.6 10.5 multiply_convert_fusion.4
  1281.7 9.2 multiply_reduce_fusion.5
  1290.9 10.5 multiply_convert_fusion.4
  1321.1 9.2 multiply_reduce_fusion.5
  1330.3 10.5 multiply_convert_fusion.4
  1378.1 157.5 %while.58 = (s32[]{:T(128)}, f32[2048,4,64]{0,2,1:T(8,128)}, f32[2048,4,64]{0,2,1:T(8,128)}, bf16[4,512,4,64]{1,3,2,0:T(8,128)(2,1)}, bf16[4,512,4,64]{1,3,2,0:T...) while((s32[]{:T(128)}, f32[2048,4,64]{0,2,1:T(8,128)}, ...), condition=%wide.region_21.21_spmd.clone, body=%wide.region_19.20_spmd.clone.sunk | while | flops 2737436672 | bytes 206102832 | solution.py:90
  1386.8 9.2 multiply_reduce_fusion.5
  1396.0 10.5 multiply_convert_fusion.4
  1426.1 9.2 multiply_reduce_fusion.5
  1435.4 10.5 multiply_convert_fusion.4
  1465.5 9.2 multiply_reduce_fusion.5
  1474.8 10.5 multiply_convert_fusion.4
  1504.9 9.2 multiply_reduce_fusion.5
  1514.1 10.5 multiply_convert_fusion.4
  1561.1 9.9 fusion.89
  1571.0 13.9 fusion.86
  1586.3 15.4 bitcast_convert_fusion
  1606.8 22.8 %all-reduce.2 = (bf16[2,256]{1,0:T(2,128)(2,1)S(1)}, bf16[1024]{0:T(1024)(128)(2,1)S(1)}) all-reduce(bf16[2,256]{1,0:T(2,128)(2,1)S(1)} %pad_maximum_fusion.7, bf16[1024]{0:T(1024)(128)(2,1)S(1)} %copy-done.45), channel_id=1, replica_groups=mesh['dp'=8,'tensor'=4] {'dp'}, use_global_device_ids=true, to_apply=%region_29.30 | all-reduce | flops 1536 | bytes 6144 | tf_op jit(solution)/shard_map/psum | solution.py:269
  1632.2 167.6 %all-reduce.6.cloned.1.call-done = (bf16[3,1024,256]{1,2,0:T(8,128)(2,1)}, bf16[256,1024]{1,0:T(8,128)(2,1)}, bf16[1024,1024]{1,0:T(8,128)(2,1)}, bf16[1024,1024]{1,0:T(8,128)(2,1)}) async-done(((bf16[3,1024,256]{1,2,0:T(8,128)(2,1)}, bf16[256,1024]{1,0:T(8,128)(2,1)}, bf16[1024,1024]{1,0:T(8,128)(2,1)}, bf16[1024,1024]{1,0:T(8,128)(2,1)}), (bf16[3,1024,256]{1,2,0:T(8,128)(2,1)}, ...) | async-done | bytes 6291472 | tf_op jit(solution)/shard_map/psum | solution.py:268
  1819.5 81.1 %reduce-scatter.11.cloned.1.call-done = bf16[3,512,1024]{2,1,0:T(8,128)(2,1)} async-done(((bf16[3,2048,1024]{2,1,0:T(8,128)(2,1)}), bf16[3,512,1024]{2,1,0:T(8,128)(2,1)}) %reduce-scatter.11.cloned.1.call-update) | async-done | bytes 3145744 | tf_op jit(solution)/shard_map/reduce_scatter | solution.py:261
  1910.6 10.3 all-reduce.1
  1920.8 37.2 %all-reduce = (f32[1024]{0:T(1024)S(1)}, f32[1024]{0:T(1024)S(1)}, f32[1024]{0:T(1024)S(1)}, f32[1024]{0:T(1024)S(1)}, f32[1024]{0:T(1024)S(1)}, /*index=5*/f32[1024]{0:T(1024)S(1)}) all-reduce(f32[1024]{0:T(1024)S(1)} %get-tuple-element.390, f32[1024]{0:T(1024)S(1)} %get-tuple-element.391, ...), channel_id=1, replica_groups=mesh['dp'=8,'tensor'=4] {'dp'}, use_global_device_ids=true, to_apply=%region_33.34 | all-reduce | flops 6144 | bytes 49152 | tf_op jit(solution)/shard_map/psum | solution.py:275
  1965.7 7.1 add_convert_fusion.1
  (503 shorter events, 590.5 us)
Async XLA Ops:
  7.2 531.8 %copy-start = (bf16[1024,1024]{1,0:T(8,128)(2,1)S(1)}, bf16[1024,1024]{1,0:T(8,128)(2,1)}, u32[]{:S(2)}) copy-start(bf16[1024,1024]{1,0:T(8,128)(2,1)} %param.34) | copy-start | bytes 6291460
  7.2 94.1 %all-gather.5.cloned.1.call-start = ((), (), s32[]{:S(2)}) async-start(), calls=%async_computation.4 | async-start | bytes 15728640 | tf_op jit(solution)/shard_map/all_gather | solution.py:136
  16.4 429.7 %reduce-scatter.5.cloned.1.call-start = ((), (), s32[]{:S(2)}) async-start(), calls=%async_computation.5 | async-start | bytes 15728640 | tf_op jit(solution)/shard_map/reduce_scatter | solution.py:156
  346.9 99.3 %copy-start.23 = (f32[1024]{0:T(1024)S(1)}, f32[1024]{0:T(1024)}, u32[]{:S(2)}) copy-start(f32[1024]{0:T(1024)} %param.33) | copy-start | bytes 12292
  346.9 106.8 %copy-start.32 = (f32[1024]{0:T(1024)S(1)}, f32[1024]{0:T(1024)}, u32[]{:S(2)}) copy-start(f32[1024]{0:T(1024)} %param.40) | copy-start | bytes 12292
  346.9 106.7 %copy-start.39 = (f32[1024]{0:T(1024)S(1)}, f32[1024]{0:T(1024)}, u32[]{:S(2)}) copy-start(f32[1024]{0:T(1024)} %param.41) | copy-start | bytes 12292
  346.9 192.0 %all-gather.7.cloned.1.call-start = ((), (), s32[]{:S(2)}) async-start(), calls=%async_computation.6 | async-start | bytes 15728640 | tf_op jit(solution)/shard_map/all_gather | solution.py:163
  456.7 82.3 %copy-start.41 = (f32[1024]{0:T(1024)S(1)}, f32[1024]{0:T(1024)}, u32[]{:S(2)}) copy-start(f32[1024]{0:T(1024)} %param.35) | copy-start | bytes 12292
  456.7 173.4 %all-gather.9.cloned.1.call-start = ((), (), s32[]{:S(2)}) async-start(), calls=%async_computation.8 | async-start | bytes 15728640 | tf_op jit(solution)/shard_map/all_gather | solution.py:185
  460.3 108.3 %copy-start.43 = (f32[3]{0:T(128)}, f32[3]{0:T(128)S(1)}, u32[]{:S(2)}) copy-start(f32[3]{0:T(128)S(1)} %dynamic_slice.47) | copy-start | bytes 40
  465.1 317.2 %reduce-scatter.9.cloned.1.call-start = ((), (), s32[]{:S(2)}) async-start(), calls=%async_computation.9 | async-start | bytes 15728640 | tf_op jit(solution)/shard_map/reduce_scatter | solution.py:212
  683.1 200.7 %reduce-scatter.7.cloned.1.call-start = ((), (), s32[]{:S(2)}) async-start(), calls=%async_computation.7 | async-start | bytes 15728640 | tf_op jit(solution)/shard_map/reduce_scatter | solution.py:181
  705.9 82.2 %copy-start.31 = (f32[3,512]{1,0:T(4,128)S(1)}, f32[3,512]{1,0:T(4,128)}, u32[]{:S(2)}) copy-start(f32[3,512]{1,0:T(4,128)} %copy-done.30) | copy-start | bytes 18436
  705.9 82.2 %copy-start.27 = (f32[3,512]{1,0:T(4,128)S(1)}, f32[3,512]{1,0:T(4,128)}, u32[]{:S(2)}) copy-start(f32[3,512]{1,0:T(4,128)} %copy-done.26) | copy-start | bytes 18436
  705.9 275.4 %all-gather.11.cloned.1.call-start = ((), (), s32[]{:S(2)}) async-start(), calls=%async_computation.10 | async-start | bytes 15728640 | tf_op jit(solution)/shard_map/all_gather | solution.py:220
  788.1 95.7 %copy-start.42 = (f32[1024]{0:T(1024)S(1)}, f32[1024]{0:T(1024)}, u32[]{:S(2)}) copy-start(f32[1024]{0:T(1024)} %param.37) | copy-start | bytes 12292
  788.1 95.7 %copy-start.44 = (f32[3]{0:T(128)S(1)}, f32[3]{0:T(128)}, u32[]{:S(2)}) copy-start(f32[3]{0:T(128)} %copy-done.43) | copy-start | bytes 40
  899.0 900.8 %all-reduce.6.cloned.1.call-start = ((), (), s32[]{:S(2)}) async-start(), calls=%async_computation.12 | async-start | bytes 12582912 | tf_op jit(solution)/shard_map/psum | solution.py:268
  918.6 62.7 %copy-start.19 = (bf16[256,1024]{1,0:T(8,128)(2,1)S(1)}, bf16[256,1024]{1,0:T(8,128)(2,1)}, u32[]{:S(2)}) copy-start(bf16[256,1024]{1,0:T(8,128)(2,1)} %param.32) | copy-start | bytes 1572868
  1019.2 9.3 copy-start.4
  1028.4 17.5 copy-start.6
  1039.0 6.9 copy-start.2
  1058.5 9.3 copy-start.4
  1067.8 17.5 copy-start.6
  1078.3 6.9 copy-start.2
  1097.9 9.3 copy-start.4
  1107.2 17.5 copy-start.6
  1117.7 6.9 copy-start.2
  1137.3 9.3 copy-start.4
  1146.6 17.5 copy-start.6
  1168.0 8.2 copy-start.5
  1202.9 9.3 copy-start.4
  1212.2 17.5 copy-start.6
  1242.3 9.3 copy-start.4
  1251.6 17.5 copy-start.6
  1281.7 9.3 copy-start.4
  1290.9 17.5 copy-start.6
  1321.1 9.3 copy-start.4
  1330.3 17.5 copy-start.6
  1351.8 8.2 copy-start.5
  1386.7 9.3 copy-start.4
  1396.0 17.5 copy-start.6
  1426.1 9.3 copy-start.4
  1435.4 17.5 copy-start.6
  1465.5 9.3 copy-start.4
  1474.8 17.5 copy-start.6
  1504.9 9.3 copy-start.4
  1514.1 17.5 copy-start.6
  1535.6 8.2 copy-start.5
  1561.1 9.9 copy-start.15
  1561.1 9.9 copy-start.16
  1561.1 9.9 copy-start.17
  1584.9 315.7 %reduce-scatter.11.cloned.1.call-start = ((), (), s32[]{:S(2)}) async-start(), calls=%async_computation.11 | async-start | bytes 15728640 | tf_op jit(solution)/shard_map/reduce_scatter | solution.py:261
  1799.8 8.3 copy-start.20
  1804.1 11.8 copy-start.18
  1809.8 90.8 %copy-start.22 = (f32[3,512]{1,0:T(4,128)S(1)}, f32[3,512]{1,0:T(4,128)}, u32[]{:S(2)}) copy-start(f32[3,512]{1,0:T(4,128)} %copy-done.21) | copy-start | bytes 18436
  1809.8 90.8 %copy-start.34 = (f32[1024]{0:T(1024)S(1)}, f32[1024]{0:T(1024)}, u32[]{:S(2)}) copy-start(f32[1024]{0:T(1024)} %param.38) | copy-start | bytes 12292
  1815.9 89.2 %copy-start.29 = (f32[3,512]{1,0:T(4,128)S(1)}, f32[3,512]{1,0:T(4,128)}, u32[]{:S(2)}) copy-start(f32[3,512]{1,0:T(4,128)} %copy-done.28) | copy-start | bytes 18436
  1815.9 89.2 %copy-start.25 = (f32[3,512]{1,0:T(4,128)S(1)}, f32[3,512]{1,0:T(4,128)}, u32[]{:S(2)}) copy-start(f32[3,512]{1,0:T(4,128)} %copy-done.24) | copy-start | bytes 18436
  1819.5 91.1 %copy-start.35 = (f32[1024]{0:T(1024)S(1)}, f32[1024]{0:T(1024)}, u32[]{:S(2)}) copy-start(f32[1024]{0:T(1024)} %get-tuple-element.318) | copy-start | bytes 12292
  1819.5 91.1 %copy-start.36 = (f32[1024]{0:T(1024)S(1)}, f32[1024]{0:T(1024)}, u32[]{:S(2)}) copy-start(f32[1024]{0:T(1024)} %get-tuple-element.314) | copy-start | bytes 12292
  1819.5 91.1 %copy-start.37 = (f32[1024]{0:T(1024)S(1)}, f32[1024]{0:T(1024)}, u32[]{:S(2)}) copy-start(f32[1024]{0:T(1024)} %get-tuple-element.402) | copy-start | bytes 12292
  1819.5 91.1 %copy-start.38 = (f32[1024]{0:T(1024)S(1)}, f32[1024]{0:T(1024)}, u32[]{:S(2)}) copy-start(f32[1024]{0:T(1024)} %get-tuple-element.417) | copy-start | bytes 12292
  1965.7 7.1 copy-start.1
  (65 other events, 232.3 us)
Sparse Core Ops, SparseCore 0:
  16.5 84.7 all-gather.4
  347.0 99.0 reduce-scatter.4
  456.8 82.0 all-gather.6
  540.4 82.0 all-gather.8
  683.2 99.0 reduce-scatter.8
  784.7 99.0 reduce-scatter.6
  899.1 82.0 all-gather.10
  1585.1 214.7 all-reduce.5
  1802.6 97.9 reduce-scatter.10
